TPU v7x, 128 devices: a whole 4x4x4 slice. The times are simulated.
128 devices in a mesh: dp: 16 (over z, y_hi, core), seq: 8 (over y_lo, x).
Axes of the slice: x: 4, y: 4 (y_hi: 2, y_lo: 2; y = y_hi * 2 + y_lo), z: 4, core: 2. Of those that a mesh axis runs over, the one named last changes fastest.
Arguments:
- tokens: bfloat16 [4096, 4096], P(('dp', 'seq')), may hold values from -6 to 6
- modality: int32 [4096], P(('dp', 'seq')), may hold values from 0 to 1, as said below
- gate_weight: bfloat16 [4096, 14336], P(None, 'dp'), may hold values from -0.09375 to 0.09375
- up_weight: bfloat16 [4096, 14336], P(None, 'dp'), may hold values from -0.09375 to 0.09375
- down_weight: bfloat16 [14336, 4096], P('dp'), may hold values from -0.046875 to 0.046875
- out_grad: bfloat16 [3072, 4096], P(('dp', 'seq')), may hold values from -1.5 to 1.5
Outputs:
- output: bfloat16 [3072, 4096], P(('dp', 'seq'))
- in_grad: bfloat16 [3072, 4096], P(('dp', 'seq'))
- gate_grad: bfloat16 [4096, 14336], P('seq', 'dp')
- up_grad: bfloat16 [4096, 14336], P('seq', 'dp')
- down_grad: bfloat16 [14336, 4096], P('dp', 'seq')
Inputs may be any that keep to these rules, and one draw needn't show every extreme that they name: In each aligned block of 32 tokens (the tokens of one device) exactly 24 tokens have modality 1 (vision); all others have 0 (text).
All inputs are finite; a program needn't handle non-finite values.
Results may differ from a plain program's by a relative error of at most 0.014.
Values may be sent and summed in bfloat16 or wider, within the bound.
A program may use at most 128 MiB of HBM per device.

v0:
```python
import jax
import jax.numpy as jnp
from jax import lax
from jax.sharding import PartitionSpec as P


def silu_parts(gate_proj):
    sigmoid_value = jax.nn.sigmoid(gate_proj)
    return (gate_proj * sigmoid_value, sigmoid_value * (1.0 + gate_proj * (1.0 - sigmoid_value)))


def contract_rows(left_matrix, right_matrix):
    return lax.dot_general(
        left_matrix, right_matrix, (((0,), (0,)), ((), ())), preferred_element_type=jnp.float32
    )


def contract_cols(left_matrix, right_matrix):
    return lax.dot_general(
        left_matrix, right_matrix, (((1,), (1,)), ((), ())), preferred_element_type=jnp.float32
    )


def on_device(tokens, modality, gate_weight, up_weight, down_weight, out_grad):
    vision_count = out_grad.shape[0]
    flags = (modality == 1).astype(jnp.int32)
    ranks = jnp.cumsum(flags) - 1
    slot_ids = jnp.arange(vision_count, dtype=jnp.int32)[:, None]
    selector = ((ranks[None, :] == slot_ids) & (flags[None, :] == 1)).astype(jnp.bfloat16)
    picked = jnp.dot(selector, tokens, preferred_element_type=jnp.float32).astype(jnp.bfloat16)
    token_rows = lax.all_gather(picked, "dp", axis=0, tiled=True)
    gate_proj = jnp.dot(token_rows, gate_weight, preferred_element_type=jnp.float32)
    up_proj = jnp.dot(token_rows, up_weight, preferred_element_type=jnp.float32)
    active, slope = silu_parts(gate_proj)
    hidden = (active * up_proj).astype(jnp.bfloat16)
    output = lax.psum_scatter(
        jnp.dot(hidden, down_weight, preferred_element_type=jnp.float32).astype(jnp.bfloat16),
        "dp",
        scatter_dimension=0,
        tiled=True,
    )
    cotangent_rows = lax.all_gather(out_grad, "dp", axis=0, tiled=True)
    back_hidden = contract_cols(cotangent_rows, down_weight)
    gate_back = (back_hidden * up_proj * slope).astype(jnp.bfloat16)
    up_back = (back_hidden * active).astype(jnp.bfloat16)
    in_grad = lax.psum_scatter(
        (contract_cols(gate_back, gate_weight) + contract_cols(up_back, up_weight)).astype(
            jnp.bfloat16
        ),
        "dp",
        scatter_dimension=0,
        tiled=True,
    )
    gate_part = contract_rows(token_rows, gate_back)
    up_part = contract_rows(token_rows, up_back)
    down_part = contract_rows(hidden, cotangent_rows)
    gate_total, up_total, down_total = (
        lax.psum_scatter(
            gate_part.astype(jnp.bfloat16), "seq", scatter_dimension=0, tiled=True
        ).astype(jnp.float32),
        lax.psum_scatter(
            up_part.astype(jnp.bfloat16), "seq", scatter_dimension=0, tiled=True
        ).astype(jnp.float32),
        lax.psum_scatter(
            down_part.astype(jnp.bfloat16), "seq", scatter_dimension=1, tiled=True
        ).astype(jnp.float32),
    )
    return (
        output,
        in_grad,
        gate_total.astype(jnp.bfloat16),
        up_total.astype(jnp.bfloat16),
        down_total.astype(jnp.bfloat16),
    )


def solution(mesh):
    placed = (
        P(("dp", "seq"), None),
        P(("dp", "seq")),
        P(None, "dp"),
        P(None, "dp"),
        P("dp", None),
        P(("dp", "seq"), None),
    )
    return jax.shard_map(
        on_device,
        mesh=mesh,
        in_specs=placed,
        out_specs=(
            P(("dp", "seq"), None),
            P(("dp", "seq"), None),
            P("seq", "dp"),
            P("seq", "dp"),
            P("dp", "seq"),
        ),
        check_vma=False,
    )
```

profile of v0, /device:TPU:1, one launch (start us, length us, event | category | flops | bytes accessed | tf_op | source)
XLA Modules:
  0.0 548.4 jit_solution(6093787396927904217)
XLA Ops:
  7.2 0.0 copy-start
  7.2 0.0 all-gather.3.cloned.1.call-start
  7.2 0.7 fusion.5
  7.9 0.1 copy.12
  8.0 0.1 reduce-window.8
  8.1 0.1 add_reduce_fusion
  8.2 0.0 copy-done
  8.2 0.9 convolution_convert_fusion.4
  9.1 0.0 all-gather.3.cloned.1.call-update
  9.1 0.0 all-gather.5.cloned.1.call-start
  9.1 0.7 all-gather.5.cloned.1.call-update
  9.8 0.0 reduce-scatter.6.cloned.1.call-start
  9.9 55.7 %all-gather.3.cloned.1.call-done = bf16[384,4096]{1,0:T(8,128)(2,1)} async-done(((bf16[24,4096]{1,0:T(8,128)(2,1)}), bf16[384,4096]{1,0:T(8,128)(2,1)}) %all-gather.3.cloned.1.call-update) | async-done | bytes 3145744 | tf_op jit(solution)/shard_map/all_gather | solution.py:31
  65.6 0.0 copy-start.2
  65.6 8.6 %fusion.8 = f32[384,896]{1,0:T(8,128)S(1)} fusion(bf16[384,4096]{1,0:T(8,128)(2,1)} %all-gather.3.cloned.1.call-done, bf16[4096,896]{1,0:T(8,128)(2,1)} %param.9), kind=kOutput, calls=%fused_computation.20 | convolution fusion | flops 2818572288 | bytes 11862016 | tf_op jit(solution)/shard_map/dot_general | solution.py:33
  74.2 0.0 copy-done.2
  74.3 5.8 %fusion.7 = f32[384,896]{1,0:T(8,128)S(1)} fusion(bf16[384,4096]{1,0:T(8,128)(2,1)S(1)} %copy-done.2, bf16[4096,896]{1,0:T(8,128)(2,1)} %param.8), kind=kOutput, calls=%fused_computation.19 | convolution fusion | flops 2818572288 | bytes 11862016 | tf_op jit(solution)/shard_map/dot_general | solution.py:32
  80.0 37.6 %all-gather.5.cloned.1.call-done = bf16[384,4096]{1,0:T(8,128)(2,1)} async-done(((bf16[24,4096]{1,0:T(8,128)(2,1)}), bf16[384,4096]{1,0:T(8,128)(2,1)}) %all-gather.5.cloned.1.call-update) | async-done | bytes 3145744 | tf_op jit(solution)/shard_map/all_gather | solution.py:42
  117.7 8.9 %multiply_convert_fusion = (bf16[384,896]{1,0:T(8,128)(2,1)}, bf16[384,896]{1,0:T(8,128)(2,1)}, bf16[384,896]{1,0:T(8,128)(2,1)S(1)}) fusion(f32[384,896]{1,0:T(8,128)S(1)} %fusion.7, f32[384,896]{1,0:T(8,128)S(1)} %fusion.8, bf16[384,4096]{1,0:T(8,128)(2,1)} %all-gather.5.cloned.1.call-done, bf16[896,4096]{1,0:T(8,128)(2,1)} %param.10), kind=kOutput, calls=%fused_computation.6 | convolution fusion | flops 2823733248 | bytes 15302656 | tf_op jit(solution)/shard_map/dot_general | solution.py:19
  126.5 0.0 copy-start.6
  126.5 0.8 copy-done.6
  127.4 8.0 %convolution_convert_fusion.3 = bf16[384,4096]{1,0:T(8,128)(2,1)} fusion(bf16[384,896]{1,0:T(8,128)(2,1)S(1)} %get-tuple-element.7, bf16[896,4096]{1,0:T(8,128)(2,1)} %param.10), kind=kOutput, calls=%fused_computation.4 | convolution fusion | flops 2820145152 | bytes 11173888 | tf_op jit(solution)/shard_map/dot_general | solution.py:37
  135.4 0.0 slice-start
  135.4 0.0 reduce-scatter.6.cloned.1.call-update
  135.5 0.0 reduce-scatter.8.cloned.1.call-start
  135.5 0.0 slice-start.1
  135.5 0.0 copy-start.5
  135.5 6.0 %fusion.9 = f32[384,4096]{1,0:T(8,128)S(1)} fusion(bf16[384,896]{1,0:T(8,128)(2,1)} %get-tuple-element.6, bf16[4096,896]{1,0:T(8,128)(2,1)} %param.8), kind=kOutput, calls=%fused_computation.21 | convolution fusion | flops 2818572288 | bytes 14319616 | tf_op jit(solution)/shard_map/dot_general | solution.py:19
  141.6 0.0 slice-done
  141.6 0.0 slice-done.1
  141.6 0.0 copy-done.5
  141.6 5.0 add_convert_fusion
  146.6 0.0 copy-start.4
  146.6 0.0 reduce-scatter.8.cloned.1.call-update
  146.6 0.2 reduce-scatter.14.cloned.1.call-start
  146.8 1.8 copy-done.4
  148.6 7.1 %convolution_convert_fusion = bf16[896,4096]{1,0:T(8,128)(2,1)} fusion(bf16[384,896]{1,0:T(8,128)(2,1)} %copy-done.6, bf16[384,4096]{1,0:T(8,128)(2,1)S(1)} %copy-done.4), kind=kOutput, calls=%fused_computation | convolution fusion | flops 2822242304 | bytes 11173888 | tf_op jit(solution)/shard_map/dot_general | solution.py:13
  155.7 0.0 copy-start.3
  155.7 0.0 reduce-scatter.14.cloned.1.call-update
  155.8 0.0 reduce-scatter.12.cloned.1.call-start
  155.8 1.9 copy-done.3
  157.7 7.5 %convolution_convert_fusion.1 = bf16[4096,896]{1,0:T(8,128)(2,1)} fusion(bf16[384,4096]{1,0:T(8,128)(2,1)S(1)} %copy-done.3, bf16[384,896]{1,0:T(8,128)(2,1)} %get-tuple-element.5), kind=kOutput, calls=%fused_computation.1 | convolution fusion | flops 2822242304 | bytes 11173888 | tf_op jit(solution)/shard_map/dot_general | solution.py:13
  165.1 0.0 reduce-scatter.12.cloned.1.call-update
  165.2 0.0 reduce-scatter.10.cloned.1.call-start
  165.2 7.5 %convolution_convert_fusion.2 = bf16[4096,896]{1,0:T(8,128)(2,1)} fusion(bf16[384,4096]{1,0:T(8,128)(2,1)S(1)} %copy-done.3, bf16[384,896]{1,0:T(8,128)(2,1)} %get-tuple-element.6), kind=kOutput, calls=%fused_computation.2 | convolution fusion | flops 2822242304 | bytes 11173888 | tf_op jit(solution)/shard_map/dot_general | solution.py:13
  172.8 0.0 copy-start.1
  172.8 0.0 reduce-scatter.10.cloned.1.call-update
  172.8 35.4 %reduce-scatter.6.cloned.1.call-done = bf16[24,4096]{1,0:T(8,128)(2,1)} async-done(((bf16[384,4096]{1,0:T(8,128)(2,1)}), bf16[24,4096]{1,0:T(8,128)(2,1)}) %reduce-scatter.6.cloned.1.call-update) | async-done | bytes 196624 | tf_op jit(solution)/shard_map/reduce_scatter | solution.py:36
  208.2 78.8 %reduce-scatter.8.cloned.1.call-done = bf16[24,4096]{1,0:T(8,128)(2,1)} async-done(((bf16[384,4096]{1,0:T(8,128)(2,1)}), bf16[24,4096]{1,0:T(8,128)(2,1)}) %reduce-scatter.8.cloned.1.call-update) | async-done | bytes 196624 | tf_op jit(solution)/shard_map/reduce_scatter | solution.py:46
  286.9 85.6 %reduce-scatter.14.cloned.1.call-done = bf16[896,512]{1,0:T(8,128)(2,1)} async-done(((bf16[896,4096]{1,0:T(8,128)(2,1)}), bf16[896,512]{1,0:T(8,128)(2,1)}) %reduce-scatter.14.cloned.1.call-update) | async-done | bytes 917520 | tf_op jit(solution)/shard_map/reduce_scatter | solution.py:64
  372.5 84.5 %reduce-scatter.12.cloned.1.call-done = bf16[512,896]{1,0:T(8,128)(2,1)} async-done(((bf16[4096,896]{1,0:T(8,128)(2,1)}), bf16[512,896]{1,0:T(8,128)(2,1)}) %reduce-scatter.12.cloned.1.call-update) | async-done | bytes 917520 | tf_op jit(solution)/shard_map/reduce_scatter | solution.py:61
  457.0 84.6 %reduce-scatter.10.cloned.1.call-done = bf16[512,896]{1,0:T(8,128)(2,1)} async-done(((bf16[4096,896]{1,0:T(8,128)(2,1)}), bf16[512,896]{1,0:T(8,128)(2,1)}) %reduce-scatter.10.cloned.1.call-update) | async-done | bytes 917520 | tf_op jit(solution)/shard_map/reduce_scatter | solution.py:58
  541.5 0.0 copy-done.1
  (1 shorter events, 0.0 us)
Async XLA Ops:
  7.2 1.0 copy-start
  7.2 58.4 %all-gather.3.cloned.1.call-start = ((), (), s32[]{:S(2)}) async-start(), calls=%async_computation.5 | async-start | bytes 3342336 | tf_op jit(solution)/shard_map/all_gather | solution.py:31
  9.1 108.6 %all-gather.5.cloned.1.call-start = ((), (), s32[]{:S(2)}) async-start(), calls=%async_computation.7 | async-start | bytes 3342336 | tf_op jit(solution)/shard_map/all_gather | solution.py:42
  9.8 198.3 %reduce-scatter.6.cloned.1.call-start = ((), (), s32[]{:S(2)}) async-start(), calls=%async_computation.6 | async-start | bytes 3342336 | tf_op jit(solution)/shard_map/reduce_scatter | solution.py:36
  65.6 8.6 %copy-start.2 = (bf16[384,4096]{1,0:T(8,128)(2,1)S(1)}, bf16[384,4096]{1,0:T(8,128)(2,1)}, u32[]{:S(2)}) copy-start(bf16[384,4096]{1,0:T(8,128)(2,1)} %all-gather.3.cloned.1.call-done) | copy-start | bytes 9437188
  126.5 0.8 copy-start.6
  135.4 6.1 %slice-start = ((s8[7340032]{0:T(1024)(128)(4,1)}), s8[3145728]{0:T(1024)(128)(4,1)S(1)}, s32[]{:S(2)}) async-start(s8[7340032]{0:T(1024)(128)(4,1)} %bitcast.21), calls=%async_computation.12 | async-start | bytes 6291456
  135.5 151.5 %reduce-scatter.8.cloned.1.call-start = ((), (), s32[]{:S(2)}) async-start(), calls=%async_computation.8 | async-start | bytes 3342336 | tf_op jit(solution)/shard_map/reduce_scatter | solution.py:46
  135.5 6.1 %slice-start.1 = ((s8[7340032]{0:T(1024)(128)(4,1)}), s8[4194304]{0:T(1024)(128)(4,1)S(1)}, s32[]{:S(2)}) async-start(s8[7340032]{0:T(1024)(128)(4,1)} %bitcast.21), calls=%async_computation.13 | async-start | bytes 8388608
  135.5 6.1 %copy-start.5 = (bf16[384,896]{1,0:T(8,128)(2,1)S(1)}, bf16[384,896]{1,0:T(8,128)(2,1)}, u32[]{:S(2)}) copy-start(bf16[384,896]{1,0:T(8,128)(2,1)} %get-tuple-element.5) | copy-start | bytes 2064388
  146.6 2.0 copy-start.4
  146.6 225.9 %reduce-scatter.14.cloned.1.call-start = ((), (), s32[]{:S(2)}) async-start(), calls=%async_computation.11 | async-start | bytes 8257536 | tf_op jit(solution)/shard_map/reduce_scatter | solution.py:64
  155.7 1.9 copy-start.3
  155.8 301.2 %reduce-scatter.12.cloned.1.call-start = ((), (), s32[]{:S(2)}) async-start(), calls=%async_computation.10 | async-start | bytes 8257536 | tf_op jit(solution)/shard_map/reduce_scatter | solution.py:61
  165.2 376.4 %reduce-scatter.10.cloned.1.call-start = ((), (), s32[]{:S(2)}) async-start(), calls=%async_computation.9 | async-start | bytes 8257536 | tf_op jit(solution)/shard_map/reduce_scatter | solution.py:58
  172.8 368.8 %copy-start.1 = (bf16[32,4096]{1,0:T(8,128)(2,1)S(1)}, bf16[32,4096]{1,0:T(8,128)(2,1)}, u32[]{:S(2)}) copy-start(bf16[32,4096]{1,0:T(8,128)(2,1)} %param.6) | copy-start | bytes 786436
Sparse Core Ops, SparseCore 0:
  11.0 54.5 all-gather.2
  68.1 49.5 all-gather.4
  135.6 72.5 reduce-scatter.5
  212.7 74.2 reduce-scatter.7
  289.8 82.6 reduce-scatter.13
  375.4 81.5 reduce-scatter.11
  460.0 81.5 reduce-scatter.9
where the time goes:
time: 549 us; the launch traced here: 548 us
  waiting for transfers between devices  463 us (84%)
  matrix products  65.3 us (12%)
  between operations  14.2 us (3%)
    reduce_scatter x1, waiting for transfers between devices, on_device(): lax.psum_scatter(down_part.astype(jnp.bfloat16), 'seq', scatter_dimension...  85.6 us
    reduce_scatter x1, waiting for transfers between devices, on_device(): lax.psum_scatter(gate_part.astype(jnp.bfloat16), 'seq', scatter_dimension...  84.6 us
    reduce_scatter x1, waiting for transfers between devices, on_device(): lax.psum_scatter(up_part.astype(jnp.bfloat16), 'seq', scatter_dimension=0...  84.5 us
    reduce_scatter x1, waiting for transfers between devices, on_device(): lax.psum_scatter((contract_cols(gate_back, gate_weight) + contract_cols(u...  78.8 us
    all_gather x1, waiting for transfers between devices, on_device(): token_rows = lax.all_gather(picked, 'dp', axis=0, tiled=True)  55.7 us
    all_gather x1, waiting for transfers between devices, on_device(): cotangent_rows = lax.all_gather(out_grad, 'dp', axis=0, tiled=True)  37.6 us
    reduce_scatter x1, waiting for transfers between devices, on_device(): lax.psum_scatter(jnp.dot(hidden, down_weight, preferred_element_type=jnp....  35.4 us
    dot_general x3, matrix products, contract_rows(): lax.dot_general(left_matrix, right_matrix, (((0,), (0,)), ((), ())), pref...  22.2 us
  transfers between devices with their start and end apart: 7, of which 7 were waited for; matrix products, arithmetic and copies ran while one was open for 9% of the time, Pallas kernels for 0%

commit v1 on v0

--- a/solution.py
+++ b/solution.py
@@ -2,6 +2,18 @@
 import jax.numpy as jnp
 from jax import lax
 from jax.sharding import PartitionSpec as P
+
+
+def list_limits(field, dim_no):
+    return jnp.concatenate(
+        lax.all_to_all(
+            jnp.stack(tuple((field for _ in range(lax.axis_size("dp"))))),
+            axis_name="dp",
+            split_axis=0,
+            concat_axis=0,
+        ),
+        axis=dim_no,
+    )
 
 
 def silu_parts(gate_proj):
@@ -39,7 +51,7 @@
         scatter_dimension=0,
         tiled=True,
     )
-    cotangent_rows = lax.all_gather(out_grad, "dp", axis=0, tiled=True)
+    cotangent_rows = list_limits(out_grad, 0)
     back_hidden = contract_cols(cotangent_rows, down_weight)
     gate_back = (back_hidden * up_proj * slope).astype(jnp.bfloat16)
     up_back = (back_hidden * active).astype(jnp.bfloat16)

time: 549 us -> 532 us (0.969)
  waiting for transfers between devices: 463 us -> 429 us
  starting transfers between devices: 0.46 us -> 9.88 us
  matrix products: 65.3 us -> 71.9 us
    all_gather x1 -> x0, waiting for transfers between devices: 37.6 us -> none  [on_device(): cotangent_rows = lax.all_gather(out_grad, 'dp', axis=0, tiled=True)]
    all_to_all x0 -> x1, starting transfers between devices: none -> 9.46 us  [list_limits(): lax.all_to_all(jnp.stack(tuple((field for _ in range(lax.axis_size('dp'))...]
    all_gather x1, waiting for transfers between devices: 55.7 us -> 63.5 us  [on_device(): token_rows = lax.all_gather(picked, 'dp', axis=0, tiled=True)]
  transfers between devices with their start and end apart: 7 -> 7, of which waited for: 7 -> 6; matrix products, arithmetic and copies ran while one was open for 9% -> 11% of each run, Pallas kernels for 0% -> 0%
where the time goes in v1:
time: 532 us
  waiting for transfers between devices  429 us (81%)
  matrix products  71.9 us (14%)
  between operations  14.2 us (3%)
  starting transfers between devices  9.88 us (2%)
  local copies, waits for them, and re-layouts  5.72 us (1%)
    reduce_scatter x1, waiting for transfers between devices, on_device(): lax.psum_scatter(down_part.astype(jnp.bfloat16), 'seq', scatter_dimension...  85.6 us
    reduce_scatter x1, waiting for transfers between devices, on_device(): lax.psum_scatter(gate_part.astype(jnp.bfloat16), 'seq', scatter_dimension...  84.4 us
    reduce_scatter x1, waiting for transfers between devices, on_device(): lax.psum_scatter(up_part.astype(jnp.bfloat16), 'seq', scatter_dimension=0...  84.4 us
    reduce_scatter x1, waiting for transfers between devices, on_device(): lax.psum_scatter((contract_cols(gate_back, gate_weight) + contract_cols(u...  78.9 us
    all_gather x1, waiting for transfers between devices, on_device(): token_rows = lax.all_gather(picked, 'dp', axis=0, tiled=True)  63.5 us
    reduce_scatter x1, waiting for transfers between devices, on_device(): lax.psum_scatter(jnp.dot(hidden, down_weight, preferred_element_type=jnp....  32.5 us
    dot_general x3, matrix products, contract_cols(): lax.dot_general(left_matrix, right_matrix, (((1,), (1,)), ((), ())), pref...  25.4 us
    dot_general x3, matrix products, contract_rows(): lax.dot_general(left_matrix, right_matrix, (((0,), (0,)), ((), ())), pref...  22.2 us
  transfers between devices with their start and end apart: 7, of which 6 were waited for; matrix products, arithmetic and copies ran while one was open for 11% of the time, Pallas kernels for 0%

profile of v1, /device:TPU:1, one launch (start us, length us, event | category | flops | bytes accessed | tf_op | source)
XLA Modules:
  0.0 531.9 jit_solution(2619268925249998542)
XLA Ops:
  7.2 0.0 copy-start
  7.2 0.0 all-gather.2.cloned.1.call-start
  7.2 0.7 fusion.5
  7.9 0.1 copy.12
  8.0 0.1 reduce-window.8
  8.1 0.1 add_reduce_fusion
  8.2 0.0 copy-done
  8.2 0.9 convolution_convert_fusion.4
  9.1 0.0 all-gather.2.cloned.1.call-update
  9.1 2.9 stack.2
  12.0 9.5 %all-to-all-start = ((bf16[16,24,4096]{2,1,0:T(8,128)(2,1)}), bf16[16,24,4096]{2,1,0:T(8,128)(2,1)S(1)}, u32[]{:S(2)}, u32[]{:S(2)}) async-start(bf16[16,24,4096]{2,1,0:T(8,128)(2,1)} %stack.2), calls=%async_computation.1 | async-start | bytes 6291456 | tf_op jit(solution)/shard_map/all_to_all | solution.py:9
  21.5 0.0 reduce-scatter.6.cloned.1.call-start
  21.5 63.5 %all-gather.2.cloned.1.call-done = bf16[384,4096]{1,0:T(8,128)(2,1)} async-done(((bf16[24,4096]{1,0:T(8,128)(2,1)}), bf16[384,4096]{1,0:T(8,128)(2,1)}) %all-gather.2.cloned.1.call-update) | async-done | bytes 3145744 | tf_op jit(solution)/shard_map/all_gather | solution.py:43
  85.0 0.0 copy-start.2
  85.0 8.7 %fusion.8 = f32[384,896]{1,0:T(8,128)} fusion(bf16[384,4096]{1,0:T(8,128)(2,1)} %all-gather.2.cloned.1.call-done, bf16[4096,896]{1,0:T(8,128)(2,1)} %param.9), kind=kOutput, calls=%fused_computation.20 | convolution fusion | flops 2818572288 | bytes 11862016 | tf_op jit(solution)/shard_map/dot_general | solution.py:45
  93.7 0.0 copy-done.2
  93.7 6.8 %fusion.7 = f32[384,896]{1,0:T(8,128)} fusion(bf16[384,4096]{1,0:T(8,128)(2,1)S(1)} %copy-done.2, bf16[4096,896]{1,0:T(8,128)(2,1)} %param.8), kind=kOutput, calls=%fused_computation.19 | convolution fusion | flops 2818572288 | bytes 11862016 | tf_op jit(solution)/shard_map/dot_general | solution.py:44
  100.5 0.0 all-to-all-done
  100.5 9.6 %multiply_convert_fusion = (bf16[384,896]{1,0:T(8,128)(2,1)}, bf16[384,896]{1,0:T(8,128)(2,1)}, bf16[384,896]{1,0:T(8,128)(2,1)S(1)}) fusion(f32[384,896]{1,0:T(8,128)} %fusion.7, f32[384,896]{1,0:T(8,128)} %fusion.8, bf16[384,4096]{1,0:T(8,128)(2,1)S(1)} %bitcast.22, bf16[896,4096]{1,0:T(8,128)(2,1)} %param.10), kind=kOutput, calls=%fused_computation.6 | convolution fusion | flops 2823733248 | bytes 15302656 | tf_op jit(solution)/shard_map/dot_general | solution.py:31
  110.1 0.0 copy-start.5
  110.1 0.8 copy-done.5
  111.0 8.0 %convolution_convert_fusion.3 = bf16[384,4096]{1,0:T(8,128)(2,1)} fusion(bf16[384,896]{1,0:T(8,128)(2,1)S(1)} %get-tuple-element.7, bf16[896,4096]{1,0:T(8,128)(2,1)} %param.10), kind=kOutput, calls=%fused_computation.4 | convolution fusion | flops 2820145152 | bytes 11173888 | tf_op jit(solution)/shard_map/dot_general | solution.py:49
  119.0 0.0 reduce-scatter.6.cloned.1.call-update
  119.0 0.0 reduce-scatter.8.cloned.1.call-start
  119.1 0.0 copy-start.4
  119.1 6.0 %fusion.9 = f32[384,4096]{1,0:T(8,128)S(1)} fusion(bf16[384,896]{1,0:T(8,128)(2,1)} %get-tuple-element.6, bf16[4096,896]{1,0:T(8,128)(2,1)} %param.8), kind=kOutput, calls=%fused_computation.21 | convolution fusion | flops 2818572288 | bytes 14319616 | tf_op jit(solution)/shard_map/dot_general | solution.py:31
  125.0 0.0 copy-done.4
  125.1 9.8 %add_convert_fusion = bf16[384,4096]{1,0:T(8,128)(2,1)} fusion(f32[384,4096]{1,0:T(8,128)S(1)} %fusion.9, bf16[384,896]{1,0:T(8,128)(2,1)S(1)} %copy-done.4, bf16[4096,896]{1,0:T(8,128)(2,1)} %param.9), kind=kOutput, calls=%fused_computation.3 | convolution fusion | flops 2821718016 | bytes 17465344 | tf_op jit(solution)/shard_map/dot_general | solution.py:31
  134.8 0.0 reduce-scatter.8.cloned.1.call-update
  134.9 0.2 reduce-scatter.14.cloned.1.call-start
  135.1 7.2 %convolution_convert_fusion = bf16[896,4096]{1,0:T(8,128)(2,1)} fusion(bf16[384,896]{1,0:T(8,128)(2,1)} %copy-done.5, bf16[384,4096]{1,0:T(8,128)(2,1)S(1)} %bitcast.23), kind=kOutput, calls=%fused_computation | convolution fusion | flops 2822242304 | bytes 11173888 | tf_op jit(solution)/shard_map/dot_general | solution.py:25
  142.2 0.0 copy-start.3
  142.2 0.0 reduce-scatter.14.cloned.1.call-update
  142.3 0.0 reduce-scatter.12.cloned.1.call-start
  142.3 1.8 copy-done.3
  144.1 7.5 %convolution_convert_fusion.1 = bf16[4096,896]{1,0:T(8,128)(2,1)} fusion(bf16[384,4096]{1,0:T(8,128)(2,1)S(1)} %copy-done.3, bf16[384,896]{1,0:T(8,128)(2,1)} %get-tuple-element.5), kind=kOutput, calls=%fused_computation.1 | convolution fusion | flops 2822242304 | bytes 11173888 | tf_op jit(solution)/shard_map/dot_general | solution.py:25
  151.6 0.0 reduce-scatter.12.cloned.1.call-update
  151.6 0.0 reduce-scatter.10.cloned.1.call-start
  151.7 7.6 %convolution_convert_fusion.2 = bf16[4096,896]{1,0:T(8,128)(2,1)} fusion(bf16[384,4096]{1,0:T(8,128)(2,1)S(1)} %copy-done.3, bf16[384,896]{1,0:T(8,128)(2,1)} %get-tuple-element.6), kind=kOutput, calls=%fused_computation.2 | convolution fusion | flops 2822242304 | bytes 11173888 | tf_op jit(solution)/shard_map/dot_general | solution.py:25
  159.2 0.0 copy-start.1
  159.2 0.0 reduce-scatter.10.cloned.1.call-update
  159.3 32.5 %reduce-scatter.6.cloned.1.call-done = bf16[24,4096]{1,0:T(8,128)(2,1)} async-done(((bf16[384,4096]{1,0:T(8,128)(2,1)}), bf16[24,4096]{1,0:T(8,128)(2,1)}) %reduce-scatter.6.cloned.1.call-update) | async-done | bytes 196624 | tf_op jit(solution)/shard_map/reduce_scatter | solution.py:48
  191.7 78.9 %reduce-scatter.8.cloned.1.call-done = bf16[24,4096]{1,0:T(8,128)(2,1)} async-done(((bf16[384,4096]{1,0:T(8,128)(2,1)}), bf16[24,4096]{1,0:T(8,128)(2,1)}) %reduce-scatter.8.cloned.1.call-update) | async-done | bytes 196624 | tf_op jit(solution)/shard_map/reduce_scatter | solution.py:58
  270.6 85.6 %reduce-scatter.14.cloned.1.call-done = bf16[896,512]{1,0:T(8,128)(2,1)} async-done(((bf16[896,4096]{1,0:T(8,128)(2,1)}), bf16[896,512]{1,0:T(8,128)(2,1)}) %reduce-scatter.14.cloned.1.call-update) | async-done | bytes 917520 | tf_op jit(solution)/shard_map/reduce_scatter | solution.py:76
  356.2 84.4 %reduce-scatter.12.cloned.1.call-done = bf16[512,896]{1,0:T(8,128)(2,1)} async-done(((bf16[4096,896]{1,0:T(8,128)(2,1)}), bf16[512,896]{1,0:T(8,128)(2,1)}) %reduce-scatter.12.cloned.1.call-update) | async-done | bytes 917520 | tf_op jit(solution)/shard_map/reduce_scatter | solution.py:73
  440.7 84.4 %reduce-scatter.10.cloned.1.call-done = bf16[512,896]{1,0:T(8,128)(2,1)} async-done(((bf16[4096,896]{1,0:T(8,128)(2,1)}), bf16[512,896]{1,0:T(8,128)(2,1)}) %reduce-scatter.10.cloned.1.call-update) | async-done | bytes 917520 | tf_op jit(solution)/shard_map/reduce_scatter | solution.py:70
  525.1 0.0 copy-done.1
Async XLA Ops:
  7.2 1.0 copy-start
  7.2 77.8 %all-gather.2.cloned.1.call-start = ((), (), s32[]{:S(2)}) async-start(), calls=%async_computation.6 | async-start | bytes 3342336 | tf_op jit(solution)/shard_map/all_gather | solution.py:43
  12.0 88.5 %all-to-all-start = ((bf16[16,24,4096]{2,1,0:T(8,128)(2,1)}), bf16[16,24,4096]{2,1,0:T(8,128)(2,1)S(1)}, u32[]{:S(2)}, u32[]{:S(2)}) async-start(bf16[16,24,4096]{2,1,0:T(8,128)(2,1)} %stack.2), calls=%async_computation.1 | async-start | bytes 6291456 | tf_op jit(solution)/shard_map/all_to_all | solution.py:9
  21.5 170.2 %reduce-scatter.6.cloned.1.call-start = ((), (), s32[]{:S(2)}) async-start(), calls=%async_computation.7 | async-start | bytes 3342336 | tf_op jit(solution)/shard_map/reduce_scatter | solution.py:48
  85.0 8.7 %copy-start.2 = (bf16[384,4096]{1,0:T(8,128)(2,1)S(1)}, bf16[384,4096]{1,0:T(8,128)(2,1)}, u32[]{:S(2)}) copy-start(bf16[384,4096]{1,0:T(8,128)(2,1)} %all-gather.2.cloned.1.call-done) | copy-start | bytes 9437188
  110.1 0.8 copy-start.5
  119.0 151.6 %reduce-scatter.8.cloned.1.call-start = ((), (), s32[]{:S(2)}) async-start(), calls=%async_computation.8 | async-start | bytes 3342336 | tf_op jit(solution)/shard_map/reduce_scatter | solution.py:58
  119.1 6.0 %copy-start.4 = (bf16[384,896]{1,0:T(8,128)(2,1)S(1)}, bf16[384,896]{1,0:T(8,128)(2,1)}, u32[]{:S(2)}) copy-start(bf16[384,896]{1,0:T(8,128)(2,1)} %get-tuple-element.5) | copy-start | bytes 2064388
  134.9 221.4 %reduce-scatter.14.cloned.1.call-start = ((), (), s32[]{:S(2)}) async-start(), calls=%async_computation.11 | async-start | bytes 8257536 | tf_op jit(solution)/shard_map/reduce_scatter | solution.py:76
  142.2 1.9 copy-start.3
  142.3 298.4 %reduce-scatter.12.cloned.1.call-start = ((), (), s32[]{:S(2)}) async-start(), calls=%async_computation.10 | async-start | bytes 8257536 | tf_op jit(solution)/shard_map/reduce_scatter | solution.py:73
  151.6 373.5 %reduce-scatter.10.cloned.1.call-start = ((), (), s32[]{:S(2)}) async-start(), calls=%async_computation.9 | async-start | bytes 8257536 | tf_op jit(solution)/shard_map/reduce_scatter | solution.py:70
  159.2 365.9 %copy-start.1 = (bf16[32,4096]{1,0:T(8,128)(2,1)S(1)}, bf16[32,4096]{1,0:T(8,128)(2,1)}, u32[]{:S(2)}) copy-start(bf16[32,4096]{1,0:T(8,128)(2,1)} %param.6) | copy-start | bytes 786436
Sparse Core Ops, SparseCore 0:
  11.0 73.9 all-gather.1
  119.1 72.5 reduce-scatter.5
  196.4 74.2 reduce-scatter.7
  273.5 82.7 reduce-scatter.13
  359.1 81.5 reduce-scatter.11
  443.5 81.5 reduce-scatter.9
